TPU v7x, 32 devices: a whole 2x2x4 slice. The times are simulated.
32 devices in a mesh: groups: 2 (over x), gx: 16 (over z, y, core).
Axes of the slice: x: 2, y: 2, z: 4, core: 2. Of those that a mesh axis runs over, the one named last changes fastest.
Arguments:
- wave_one: float32 [2, 512, 2048], P(None, 'groups', 'gx'), parts along dimension 1, may hold values from -6 to 6
- wave_two: float32 [2, 512, 2048], P(None, 'groups', 'gx'), parts along dimension 1, may hold values from -4.2 to 4.2
- mismatch: float32 [512, 2048], P('groups', 'gx'), parts along dimension 0, may hold values from -1.2 to 1.2
- plate: int32 [16, 64], P('groups', 'gx'), parts along dimension 0, may hold values from 0 to 15
- spot_low: int32 [1024], P('groups'), parts along dimension 0, may hold values from 64 to 255
- spot_high: int32 [1024], P('groups'), parts along dimension 0, may hold values from 256 to 447
- row_gain: float32 [1024], P('groups'), parts along dimension 0, may hold values from 0.5 to 3
- column_gain: float32 [1024], P('groups'), parts along dimension 0, may hold values from 0.5 to 3
Outputs:
- third: float32 [2, 512, 2048], P(None, 'groups', 'gx'), parts along dimension 1
- far_field: float32 [2, 1024, 512], P(None, ('groups', 'gx')), parts along dimension 1
- back_field: float32 [2, 512, 2048], P(None, 'groups', 'gx'), parts along dimension 1
There are 2 independent parts, one for each index of `groups`. A program takes and returns all parts, laid end to end along the dimension named above; each array names one. Nothing has to cross between parts.
All inputs are finite; a program needn't handle non-finite values.
Results may differ from a plain program's by a relative error of at most 0.00017.
Values sent between devices are 32-bit elements; how exact they have to be, the bound alone decides.
A program may use at most 64 MiB of HBM per device.

v0:
```python
import math

import jax
import jax.numpy as jnp
import numpy as np
from jax import lax
from jax.experimental import pallas as pl
from jax.experimental.pallas import tpu as pltpu
from jax.sharding import PartitionSpec as P

SUBSTEPS = 4
ZOOM = 4
LEVELS = 16
PLATE = 32

DIFFRACT = (0.08, 0.04, 0.027)
WALKOFF = (0.3, -0.8, 0.8)
COUPLE = (0.08, 0.16, 0.24)
FAR_SCALE = 4.0
HALO = 2 * SUBSTEPS
PAD = 8
TILE = 16
MESH = pl.DeviceIdType.MESH


def split_host(array):
    high = array.astype(jnp.bfloat16)
    low = (array - high.astype(np.float64)).astype(jnp.bfloat16)
    return high, low


def split(value):
    high = value.astype(jnp.bfloat16)
    low = (value - high.astype(jnp.float32)).astype(jnp.bfloat16)
    return high, low


def dot(left, right, transposed=False):
    contract = ((1,), (1,)) if transposed else ((1,), (0,))
    return lax.dot_general(
        left, right, (contract, ((), ())), preferred_element_type=jnp.float32
    )


def dot3(left, right, transposed=False):
    return (
        dot(left[0], right[0], transposed)
        + dot(left[1], right[0], transposed)
        + dot(left[0], right[1], transposed)
    )


def sine_cosine(angle):
    square = angle * angle
    sine = 1.0
    for term in (11, 9, 7, 5, 3):
        sine = 1.0 - square * (1.0 / (term * (term - 1))) * sine
    cosine = 1.0
    for term in (12, 10, 8, 6, 4, 2):
        cosine = 1.0 - square * (1.0 / (term * (term - 1))) * cosine
    return angle * sine, cosine


def rates(window, turn):
    current, laplace, moving = [], [], []
    rows = TILE
    for channel in range(6):
        block = window[channel]
        whole = block.shape[0]
        width = block.shape[1]
        cur = block[8 : 8 + rows]
        left = pltpu.roll(block, 1, 0)[8 : 8 + rows]
        right = pltpu.roll(block, whole - 1, 0)[8 : 8 + rows]
        lane = lax.broadcasted_iota(jnp.int32, cur.shape, 1)
        above = jnp.where(lane == 0, 0.0, pltpu.roll(cur, 1, 1))
        below = jnp.where(lane == width - 1, 0.0, pltpu.roll(cur, width - 1, 1))
        drift = WALKOFF[channel // 2]
        current.append(cur)
        laplace.append(above + below + left + right - 4.0 * cur)
        if drift > 0:
            moving.append(-drift * (cur - left))
        else:
            moving.append(-drift * (right - cur))
    a1r, a1i, a2r, a2i, a3r, a3i = current
    pr = a1r * a2r - a1i * a2i
    pi = a1r * a2i + a1i * a2r
    if turn is None:
        br, bi = a3r, a3i
        m3r, m3i = pr, pi
    else:
        cosine, sine = turn
        br = a3r * cosine + a3i * sine
        bi = a3i * cosine - a3r * sine
        m3r = pr * cosine - pi * sine
        m3i = pi * cosine + pr * sine
    mixing = (
        (br * a2r + bi * a2i, bi * a2r - br * a2i),
        (br * a1r + bi * a1i, bi * a1r - br * a1i),
        (m3r, m3i),
    )
    result = []
    for wave in range(3):
        spread, strength = DIFFRACT[wave], COUPLE[wave]
        mr, mi = mixing[wave]
        result.append(moving[2 * wave] - spread * laplace[2 * wave + 1] - strength * mi)
        result.append(moving[2 * wave + 1] + spread * laplace[2 * wave] + strength * mr)
    return current, result


def kernel(
    devices,
    w1_ref,
    w2_ref,
    mis_ref,
    plate_ref,
    low_ref,
    high_ref,
    rgain_ref,
    cgain_ref,
    lhigh_hbm,
    llow_hbm,
    thigh_hbm,
    tlow_hbm,
    shigh_hbm,
    slow_hbm,
    third_ref,
    far_ref,
    back_ref,
    lhigh,
    llow,
    thigh,
    tlow,
    shigh,
    slow,
    fields,
    trial,
    turns,
    edge_out,
    edge_in,
    mis_wide,
    g_out,
    g_in,
    h_out,
    h_in,
    table_sem,
    edge_send,
    edge_recv,
    g_send,
    g_recv,
    h_send,
    h_recv,
):
    me = lax.axis_index("gx")
    row_count, width_here = mis_ref.shape
    far_rows = rgain_ref.shape[1]
    far_columns = cgain_ref.shape[1]
    block = far_rows // devices
    classes = far_columns // width_here
    scale = FAR_SCALE / math.sqrt(row_count * width_here * devices)
    wide = width_here + 2 * HALO
    tiles = wide // TILE

    def place(index):
        return (index - devices // 2 + classes // 2) % classes

    tables = [
        pltpu.make_async_copy(src, dst, table_sem.at[i])
        for i, (src, dst) in enumerate(
            (
                (lhigh_hbm, lhigh),
                (llow_hbm, llow),
                (shigh_hbm, shigh),
                (slow_hbm, slow),
                (thigh_hbm, thigh),
                (tlow_hbm, tlow),
            )
        )
    ]
    for copy in tables:
        copy.start()

    barrier = pltpu.get_barrier_semaphore()

    @pl.loop(1, devices)
    def _(k):
        pl.semaphore_signal(
            barrier, inc=1, device_id={"gx": lax.rem(me + k, devices)}, device_id_type=MESH
        )

    planes = [w1_ref[0], w1_ref[1], w2_ref[0], w2_ref[1], mis_ref[...]]
    own = PAD + HALO
    for plane, value in enumerate(planes):
        turned = value.T
        edge_out[0, plane * HALO : (plane + 1) * HALO, :] = turned[:HALO]
        edge_out[1, plane * HALO : (plane + 1) * HALO, :] = turned[width_here - HALO :]
        if plane < 4:
            fields[plane, own : own + width_here, :] = turned
        else:
            mis_wide[HALO : HALO + width_here, :] = turned
    for plane in (4, 5):
        fields[plane] = jnp.zeros(fields.shape[1:], jnp.float32)
    edge = jnp.zeros((PAD, row_count), jnp.float32)
    for plane in range(6):
        for start in (0, PAD + wide):
            fields[plane, start : start + PAD, :] = edge
            trial[plane, start : start + PAD, :] = edge

    pl.semaphore_wait(barrier, devices - 1)

    def edge_copy(side):
        return pltpu.make_async_remote_copy(
            src_ref=edge_out.at[side],
            dst_ref=edge_in.at[1 - side],
            send_sem=edge_send.at[side],
            recv_sem=edge_recv.at[1 - side],
            device_id={"gx": me - 1 if side == 0 else me + 1},
            device_id_type=MESH,
        )

    @pl.when(me > 0)
    def _():
        edge_copy(0).start()

    @pl.when(me < devices - 1)
    def _():
        edge_copy(1).start()

    @pl.when(me > 0)
    def _():
        edge_copy(1).wait_recv()

    @pl.when(me == 0)
    def _():
        edge_in[0] = jnp.zeros(edge_in.shape[1:], jnp.float32)

    @pl.when(me < devices - 1)
    def _():
        edge_copy(0).wait_recv()

    @pl.when(me == devices - 1)
    def _():
        edge_in[1] = jnp.zeros(edge_in.shape[1:], jnp.float32)

    for side, start in ((0, 0), (1, HALO + width_here)):
        for plane in range(5):
            value = edge_in[side, plane * HALO : (plane + 1) * HALO, :]
            if plane < 4:
                fields[plane, PAD + start : PAD + start + HALO, :] = value
            else:
                mis_wide[start : start + HALO, :] = value

    @pl.loop(0, tiles)
    def _(t):
        here = pl.ds(pl.multiple_of(t * TILE, TILE), TILE)
        sine, cosine = sine_cosine(mis_wide[here, :])
        c2 = cosine * cosine - sine * sine
        s2 = 2.0 * sine * cosine
        powers = (
            (cosine, sine),
            (c2, s2),
            (c2 * cosine - s2 * sine, s2 * cosine + c2 * sine),
            (c2 * c2 - s2 * s2, 2.0 * s2 * c2),
        )
        for z, (c, s) in enumerate(powers):
            turns[z, 0, here, :] = c
            turns[z, 1, here, :] = s

    lowest = jnp.where(me == 0, HALO, 0)
    highest = jnp.where(me == devices - 1, HALO + width_here, wide)

    def stage(source, position, finish):
        @pl.loop(0, tiles)
        def _(t):
            first = pl.multiple_of(t * TILE, 8)
            here = pl.ds(pl.multiple_of(first + PAD, 8), TILE)
            window = [source[c, pl.ds(first, TILE + 16), :] for c in range(6)]
            turn = None
            if position:
                at = pl.ds(first, TILE)
                turn = (turns[position - 1, 0, at, :], turns[position - 1, 1, at, :])
            current, rate = rates(window, turn)
            row = first + lax.broadcasted_iota(jnp.int32, current[0].shape, 0)
            inside = (row >= lowest) & (row < highest)
            for c in range(6):
                finish(c, here, current[c], rate[c], inside)

    for substep in range(SUBSTEPS):

        def predict(c, here, current, rate, inside):
            trial[c, here, :] = jnp.where(inside, current + rate, 0.0)

        def correct(c, here, current, rate, inside):
            value = 0.5 * (fields[c, here, :] + (current + rate))
            fields[c, here, :] = jnp.where(inside, value, 0.0)

        stage(fields, substep, predict)
        stage(trial, substep + 1, correct)

    step = 2.0 * math.pi / LEVELS
    plate_rows, plate_columns = plate_ref.shape

    def phases(shape, rows_first):
        sub = lax.broadcasted_iota(jnp.int32, shape, 0)
        lane = lax.broadcasted_iota(jnp.int32, shape, 1) // PLATE
        level = jnp.zeros(shape, jnp.int32)
        for r in range(plate_rows):
            for c in range(plate_columns):
                at = (sub == r) & (lane == c) if rows_first else (sub == c) & (lane == r)
                level = jnp.where(at, plate_ref[r, c], level)
        angle = step * level.astype(jnp.float32)
        return jnp.cos(angle), jnp.sin(angle)

    def spread(value, count):
        return jnp.concatenate(
            [
                jnp.broadcast_to(value[i : i + 1], (PLATE, value.shape[1]))
                for i in range(count)
            ],
            axis=0,
        )

    across = phases((max(8, plate_columns), row_count), False)
    cosine, sine = (spread(v, plate_columns) for v in across)
    tr = fields[4, own : own + width_here, :]
    ti = fields[5, own : own + width_here, :]
    nr = tr * cosine - ti * sine
    ni = tr * sine + ti * cosine
    near = split(
        jnp.concatenate(
            [
                jnp.concatenate([nr, ni], axis=1),
                jnp.concatenate([ni, -nr], axis=1),
            ],
            axis=0,
        )
    )
    tables[0].wait()
    tables[1].wait()
    chunks = max(1, far_rows // 128)
    chunk = far_rows // chunks
    per = chunk // block
    for n in range(chunks):
        at = slice(n * chunk, (n + 1) * chunk)
        g = dot3((lhigh[at, :], llow[at, :]), near, True)
        for j in range(per):
            rows = slice(j * block, (j + 1) * block)
            g_out[n * per + j, :block, :] = g[rows, :width_here]
            g_out[n * per + j, block:, :] = g[rows, width_here:]

    def g_copy(target, source):
        return pltpu.make_async_remote_copy(
            src_ref=g_out.at[target],
            dst_ref=g_in.at[source],
            send_sem=g_send.at[target],
            recv_sem=g_recv.at[source],
            device_id={"gx": target},
            device_id_type=MESH,
        )

    @pl.loop(1, devices)
    def _(k):
        g_copy(lax.rem(me + k, devices), me).start()

    g_in[me] = g_out[me]
    third_ref[0] = tr.T
    third_ref[1] = ti.T

    lane = lax.broadcasted_iota(jnp.int32, (block, far_rows), 1)
    row = me * block + lax.broadcasted_iota(jnp.int32, (block, far_rows), 0)

    def pick(ref):
        value = jnp.broadcast_to(ref[...].astype(jnp.float32), (block, far_rows))
        return jnp.sum(jnp.where(lane == row, value, 0.0), axis=1, keepdims=True)

    spot_low, spot_high, row_gain = pick(low_ref), pick(high_ref), pick(rgain_ref)
    gain = row_gain * cgain_ref[...]

    tables[2].wait()
    tables[3].wait()

    @pl.loop(1, devices)
    def _(k):
        source = lax.rem(me + k, devices)
        g_copy(source, source).wait_recv()

    folded = []
    for position in range(classes):
        total = None
        for source in range(devices):
            if place(source) == position:
                total = g_in[source] if total is None else total + g_in[source]
        folded.append(total)
    spectrum = dot3(split(jnp.concatenate(folded, axis=1)), (shigh[...], slow[...]))
    far_r = scale * (spectrum[:block, :far_columns] + spectrum[block:, far_columns:])
    far_i = scale * (spectrum[block:, :far_columns] - spectrum[:block, far_columns:])
    far_ref[0] = far_r
    far_ref[1] = far_i
    magnitude = jnp.sqrt(far_r * far_r + far_i * far_i)
    column = lax.broadcasted_iota(jnp.int32, far_r.shape, 1).astype(jnp.float32)
    inside = (column >= spot_low) & (column < spot_high)
    factor = jnp.where(inside, gain / jnp.maximum(magnitude, 1.0), 1.0)
    replaced = split(jnp.concatenate([far_r * factor, far_i * factor], axis=0))
    turned = dot3(replaced, (shigh[...], slow[...]))
    hr = turned[:block, :far_columns] - turned[block:, far_columns:]
    hi = turned[block:, :far_columns] + turned[:block, far_columns:]
    for position in range(classes):
        at = slice(position * width_here, (position + 1) * width_here)
        h_out[position, :block, :] = hr[:, at]
        h_out[position, block:, :] = hi[:, at]

    def h_copy(target, source):
        return pltpu.make_async_remote_copy(
            src_ref=h_out.at[place(target)],
            dst_ref=h_in.at[source],
            send_sem=h_send.at[target],
            recv_sem=h_recv.at[source],
            device_id={"gx": target},
            device_id_type=MESH,
        )

    @pl.loop(1, devices)
    def _(k):
        h_copy(lax.rem(me + k, devices), me).start()

    h_in[me] = h_out[place(me)]
    down = phases((max(8, plate_rows), width_here), True)
    cosine, sine = (spread(v, plate_rows) for v in down)
    tables[4].wait()
    tables[5].wait()

    @pl.loop(1, devices)
    def _(k):
        source = lax.rem(me + k, devices)
        h_copy(source, source).wait_recv()

    gathered = jnp.concatenate(
        [
            jnp.concatenate([h_in[s, :block, :], h_in[s, block:, :]], axis=1)
            for s in range(devices)
        ],
        axis=0,
    )
    summed = dot3((thigh[...], tlow[...]), split(gathered))
    br = scale * (summed[:row_count, :width_here] - summed[row_count:, width_here:])
    bi = scale * (summed[:row_count, width_here:] + summed[row_count:, :width_here])
    back_ref[0] = br * cosine + bi * sine
    back_ref[1] = bi * cosine - br * sine

    @pl.when(me > 0)
    def _():
        edge_copy(0).wait_send()

    @pl.when(me < devices - 1)
    def _():
        edge_copy(1).wait_send()

    @pl.loop(1, devices)
    def _(k):
        target = lax.rem(me + k, devices)
        g_copy(target, me).wait_send()
        h_copy(target, me).wait_send()


def local(wave_one, wave_two, mismatch, plate, spot_low, spot_high, row_gain, column_gain):
    devices = lax.axis_size("gx")
    row_count, width_here = mismatch.shape
    far_rows = row_gain.shape[0]
    far_columns = column_gain.shape[0]
    block = far_rows // devices
    classes = far_columns // width_here

    def angle_table(first, second, period):
        turns = np.mod(first[:, None] * second[None, :], period)
        angle = 2.0 * np.pi / period * turns
        return np.cos(angle), np.sin(angle)

    row_table = np.concatenate(
        angle_table(
            np.arange(far_rows) - far_rows // 2,
            np.arange(row_count) - row_count // 2,
            ZOOM * row_count,
        ),
        axis=1,
    )
    around = np.arange(far_columns) - far_columns // 2
    column_table = np.concatenate(angle_table(around, around, far_columns), axis=1)
    tables = (
        *split_host(row_table),
        *split_host(row_table.T),
        *split_host(column_table),
    )
    tables = [jnp.asarray(t) for t in tables]
    wide = width_here + 2 * HALO
    vmem = pl.BlockSpec(memory_space=pltpu.VMEM)
    smem = pl.BlockSpec(memory_space=pltpu.SMEM)
    anywhere = pl.BlockSpec(memory_space=pl.ANY)
    f32 = jnp.float32
    dma = pltpu.SemaphoreType.DMA

    def body(*refs):
        kernel(devices, *refs)

    return pl.pallas_call(
        body,
        out_shape=(
            jax.ShapeDtypeStruct((2, row_count, width_here), f32),
            jax.ShapeDtypeStruct((2, block, far_columns), f32),
            jax.ShapeDtypeStruct((2, row_count, width_here), f32),
        ),
        in_specs=[vmem] * 3 + [smem] + [vmem] * 4 + [anywhere] * 6,
        out_specs=(vmem,) * 3,
        scratch_shapes=[
            *[pltpu.VMEM(t.shape, t.dtype) for t in tables],
            pltpu.VMEM((6, wide + 2 * PAD, row_count), f32),
            pltpu.VMEM((6, wide + 2 * PAD, row_count), f32),
            pltpu.VMEM((SUBSTEPS, 2, wide, row_count), f32),
            pltpu.VMEM((2, 5 * HALO, row_count), f32),
            pltpu.VMEM((2, 5 * HALO, row_count), f32),
            pltpu.VMEM((wide, row_count), f32),
            pltpu.VMEM((devices, 2 * block, width_here), f32),
            pltpu.VMEM((devices, 2 * block, width_here), f32),
            pltpu.VMEM((classes, 2 * block, width_here), f32),
            pltpu.VMEM((devices, 2 * block, width_here), f32),
            dma((6,)),
            dma((2,)),
            dma((2,)),
            dma((devices,)),
            dma((devices,)),
            dma((devices,)),
            dma((devices,)),
        ],
        compiler_params=pltpu.CompilerParams(
            collective_id=0, has_side_effects=True, vmem_limit_bytes=48 * 1024 * 1024
        ),
    )(
        wave_one,
        wave_two,
        mismatch,
        plate,
        spot_low[None],
        spot_high[None],
        row_gain[None],
        column_gain[None],
        *tables,
    )


def solution(mesh):
    return jax.shard_map(
        local,
        mesh=mesh,
        in_specs=(
            P(None, "groups", "gx"),
            P(None, "groups", "gx"),
            P("groups", "gx"),
            P("groups", "gx"),
            P("groups"),
            P("groups"),
            P("groups"),
            P("groups"),
        ),
        out_specs=(
            P(None, "groups", "gx"),
            P(None, ("groups", "gx"), None),
            P(None, "groups", "gx"),
        ),
        check_vma=False,
    )
```

profile of v0, /device:TPU:13, one launch (start us, length us, event | category | flops | bytes accessed | tf_op | source)
XLA Modules:
  0.0 59.2 jit_solution(9811577100001962444)
XLA Ops:
  0.6 0.0 copy-start.13
  0.6 0.0 copy-start.12
  0.7 0.7 %copy-done.13 = s32[8,4]{0,1:T(4,128)S(1)} copy-done((s32[8,4]{0,1:T(4,128)S(1)}, s32[8,4]{0,1:T(4,128)}, u32[]{:S(2)}) %copy-start.13) | copy-done | bytes 152
  1.3 0.0 copy-start.9
  1.3 0.0 copy-start.10
  1.3 0.0 copy-start.11
  1.3 0.1 copy.17.refs_3_
  1.4 0.0 copy-done.12
  1.4 0.6 copy-done.9
  2.0 0.0 copy-done.10
  2.0 0.0 copy-done.11
  2.0 1.2 %copy-done = bf16[512,1024]{1,0:T(8,128)(2,1)S(1)} copy-done((bf16[512,1024]{1,0:T(8,128)(2,1)S(1)}, bf16[512,1024]{1,0:T(8,128)(2,1)}, u32[]{:S(2)}) %copy-start) | copy-done | bytes 1048600
  3.3 1.2 %copy-done.1 = bf16[512,1024]{1,0:T(8,128)(2,1)S(1)} copy-done((bf16[512,1024]{1,0:T(8,128)(2,1)S(1)}, bf16[512,1024]{1,0:T(8,128)(2,1)}, u32[]{:S(2)}) %copy-start.1) | copy-done | bytes 1048600
  4.5 1.0 %copy-done.2 = bf16[512,512]{1,0:T(8,128)(2,1)S(1)} copy-done((bf16[512,512]{1,0:T(8,128)(2,1)S(1)}, bf16[512,512]{1,0:T(8,128)(2,1)}, u32[]{:S(2)}) %copy-start.2) | copy-done | bytes 524312
  5.5 1.0 %copy-done.3 = bf16[512,512]{1,0:T(8,128)(2,1)S(1)} copy-done((bf16[512,512]{1,0:T(8,128)(2,1)S(1)}, bf16[512,512]{1,0:T(8,128)(2,1)}, u32[]{:S(2)}) %copy-start.3) | copy-done | bytes 524312
  6.6 1.0 %copy-done.4 = bf16[512,512]{1,0:T(8,128)(2,1)S(1)} copy-done((bf16[512,512]{1,0:T(8,128)(2,1)S(1)}, bf16[512,512]{1,0:T(8,128)(2,1)}, u32[]{:S(2)}) %copy-start.4) | copy-done | bytes 524312
  7.6 1.0 %copy-done.5 = bf16[512,512]{1,0:T(8,128)(2,1)S(1)} copy-done((bf16[512,512]{1,0:T(8,128)(2,1)S(1)}, bf16[512,512]{1,0:T(8,128)(2,1)}, u32[]{:S(2)}) %copy-start.5) | copy-done | bytes 524312
  8.6 0.9 %copy-done.6 = f32[2,256,128]{2,1,0:T(8,128)S(1)} copy-done((f32[2,256,128]{2,1,0:T(8,128)S(1)}, f32[2,256,128]{2,1,0:T(8,128)}, u32[]{:S(2)}) %copy-start.6) | copy-done | bytes 262168
  9.6 0.9 %copy-done.7 = f32[2,256,128]{2,1,0:T(8,128)S(1)} copy-done((f32[2,256,128]{2,1,0:T(8,128)S(1)}, f32[2,256,128]{2,1,0:T(8,128)}, u32[]{:S(2)}) %copy-start.7) | copy-done | bytes 262168
  10.6 0.9 %copy-done.8 = f32[256,128]{1,0:T(8,128)S(1)} copy-done((f32[256,128]{1,0:T(8,128)S(1)}, f32[256,128]{1,0:T(8,128)}, u32[]{:S(2)}) %copy-start.8) | copy-done | bytes 131096
  11.5 45.7 %shard_map.157 = (f32[2,256,128]{2,1,0:T(8,128)S(1)}, f32[2,32,512]{2,1,0:T(8,128)S(1)}, f32[2,256,128]{2,1,0:T(8,128)S(1)}) custom-call(f32[2,256,128]{2,1,0:T(8,128)S(1)} %copy-done.6, f32[2,256,128]{2,1,0:T(8,128)S(1)} %copy-done.7, f32[256,128]{1,0:T(8,128)S(1)} %copy-done.8, s32[8,4]{1,0:T(8,128)S(1)} %copy.17.refs_3_, s32[1,512]{1,0:T(1,128)S(1)} %bitcast.4, ...), custom_call_target="tpu_custom_call" | custom-call | tf_op jit(solution)/shard_map/pallas_call | solution.py:503
  57.1 0.7 %copy.21 = f32[2,256,128]{2,1,0:T(8,128)} copy(f32[2,256,128]{2,1,0:T(8,128)S(1)} %get-tuple-element.6) | data formatting | bytes 524288
  57.8 0.7 %copy.22 = f32[2,32,512]{2,1,0:T(8,128)} copy(f32[2,32,512]{2,1,0:T(8,128)S(1)} %get-tuple-element.7) | data formatting | bytes 262144
  58.5 0.7 %copy.23 = f32[2,256,128]{2,1,0:T(8,128)} copy(f32[2,256,128]{2,1,0:T(8,128)S(1)} %get-tuple-element.8) | data formatting | bytes 524288
  (9 shorter events, 0.0 us)
Async XLA Ops:
  0.6 0.7 %copy-start.13 = (s32[8,4]{0,1:T(4,128)S(1)}, s32[8,4]{0,1:T(4,128)}, u32[]{:S(2)}) copy-start(s32[8,4]{0,1:T(4,128)} %param.17) | copy-start | bytes 388
  0.6 0.8 %copy-start.12 = (f32[512]{0:T(512)S(1)}, f32[512]{0:T(512)}, u32[]{:S(2)}) copy-start(f32[512]{0:T(512)} %param.21) | copy-start | bytes 6148
  1.3 0.7 %copy-start.9 = (s32[512]{0:T(512)S(1)}, s32[512]{0:T(512)}, u32[]{:S(2)}) copy-start(s32[512]{0:T(512)} %param.18) | copy-start | bytes 6148
  1.3 0.7 %copy-start.10 = (s32[512]{0:T(512)S(1)}, s32[512]{0:T(512)}, u32[]{:S(2)}) copy-start(s32[512]{0:T(512)} %param.19) | copy-start | bytes 6148
  1.3 0.7 %copy-start.11 = (f32[512]{0:T(512)S(1)}, f32[512]{0:T(512)}, u32[]{:S(2)}) copy-start(f32[512]{0:T(512)} %param.20) | copy-start | bytes 6148
  2.0 1.2 %copy-start = (bf16[512,1024]{1,0:T(8,128)(2,1)S(1)}, bf16[512,1024]{1,0:T(8,128)(2,1)}, u32[]{:S(2)}) copy-start(bf16[512,1024]{1,0:T(8,128)(2,1)} %constant.17.clone.refs_13_) | copy-start | bytes 3145732
  3.3 1.2 %copy-start.1 = (bf16[512,1024]{1,0:T(8,128)(2,1)S(1)}, bf16[512,1024]{1,0:T(8,128)(2,1)}, u32[]{:S(2)}) copy-start(bf16[512,1024]{1,0:T(8,128)(2,1)} %constant.16.clone.refs_12_) | copy-start | bytes 3145732
  4.5 1.0 %copy-start.2 = (bf16[512,512]{1,0:T(8,128)(2,1)S(1)}, bf16[512,512]{1,0:T(8,128)(2,1)}, u32[]{:S(2)}) copy-start(bf16[512,512]{1,0:T(8,128)(2,1)} %constant.15.clone.refs_11_) | copy-start | bytes 1572868
  5.5 1.0 %copy-start.3 = (bf16[512,512]{1,0:T(8,128)(2,1)S(1)}, bf16[512,512]{1,0:T(8,128)(2,1)}, u32[]{:S(2)}) copy-start(bf16[512,512]{1,0:T(8,128)(2,1)} %constant.14.clone.refs_10_) | copy-start | bytes 1572868
  6.6 1.0 %copy-start.4 = (bf16[512,512]{1,0:T(8,128)(2,1)S(1)}, bf16[512,512]{1,0:T(8,128)(2,1)}, u32[]{:S(2)}) copy-start(bf16[512,512]{1,0:T(8,128)(2,1)} %constant.13.clone.refs_9_) | copy-start | bytes 1572868
  7.6 1.0 %copy-start.5 = (bf16[512,512]{1,0:T(8,128)(2,1)S(1)}, bf16[512,512]{1,0:T(8,128)(2,1)}, u32[]{:S(2)}) copy-start(bf16[512,512]{1,0:T(8,128)(2,1)} %constant.12.clone.refs_8_) | copy-start | bytes 1572868
  8.6 0.9 %copy-start.6 = (f32[2,256,128]{2,1,0:T(8,128)S(1)}, f32[2,256,128]{2,1,0:T(8,128)}, u32[]{:S(2)}) copy-start(f32[2,256,128]{2,1,0:T(8,128)} %refs_0_.1) | copy-start | bytes 786436
  9.6 0.9 %copy-start.7 = (f32[2,256,128]{2,1,0:T(8,128)S(1)}, f32[2,256,128]{2,1,0:T(8,128)}, u32[]{:S(2)}) copy-start(f32[2,256,128]{2,1,0:T(8,128)} %refs_1_.1) | copy-start | bytes 786436
  10.5 0.9 %copy-start.8 = (f32[256,128]{1,0:T(8,128)S(1)}, f32[256,128]{1,0:T(8,128)}, u32[]{:S(2)}) copy-start(f32[256,128]{1,0:T(8,128)} %refs_2_.1) | copy-start | bytes 393220
where the time goes:
time: 60.1 us; the launch traced here: 59.2 us
  Pallas kernels  45.7 us (76%)
  local copies, waits for them, and re-layouts  12.9 us (21%)
  between operations  0.67 us (1%)
    pallas_call x1, Pallas kernels, local(): pl.pallas_call(body, out_shape=(jax.ShapeDtypeStruct((2, row_count, width...  45.7 us
    unnamed x32, local copies, waits for them, and re-layouts  12.9 us

commit v1 on v0

--- a/solution.py
+++ b/solution.py
@@ -2,7 +2,6 @@
 
 import jax
 import jax.numpy as jnp
-import numpy as np
 from jax import lax
 from jax.experimental import pallas as pl
 from jax.experimental.pallas import tpu as pltpu
@@ -21,12 +20,6 @@
 PAD = 8
 TILE = 16
 MESH = pl.DeviceIdType.MESH
-
-
-def split_host(array):
-    high = array.astype(jnp.bfloat16)
-    low = (array - high.astype(np.float64)).astype(jnp.bfloat16)
-    return high, low
 
 
 def split(value):
@@ -61,11 +54,43 @@
     return angle * sine, cosine
 
 
-def rates(window, turn):
+def wave_table(high, low, rows, lanes, shifts, period, sine_at):
+    shape = (TILE, lanes)
+    lane = lax.broadcasted_iota(jnp.int32, shape, 1) - shifts[1]
+    row = lax.broadcasted_iota(jnp.int32, shape, 0) - shifts[0]
+
+    def turn(product):
+        angle = (2.0 * math.pi / period) * (product & (period - 1)).astype(jnp.float32)
+        return jnp.cos(angle), jnp.sin(angle)
+
+    first = turn(row * lane)
+    step = turn(TILE * lane[:8])
+    step = [jnp.concatenate([v, v], axis=0) for v in step]
+
+    def body(i, carry):
+        at = pl.multiple_of(i * TILE, TILE)
+        for value, (down, across) in zip(carry, ((0, 0), sine_at)):
+            here = (pl.ds(pl.multiple_of(at + down, TILE), TILE), slice(across, across + lanes))
+            high[here], low[here] = split(value)
+        cosine, sine = carry
+        return (
+            cosine * step[0] - sine * step[1],
+            sine * step[0] + cosine * step[1],
+        )
+
+    lax.fori_loop(0, rows // TILE, body, first)
+
+
+def rates(window, turn, only_third):
     current, laplace, moving = [], [], []
     rows = TILE
     for channel in range(6):
         block = window[channel]
+        if only_third and channel < 4:
+            current.append(block[8 : 8 + rows])
+            laplace.append(None)
+            moving.append(None)
+            continue
         whole = block.shape[0]
         width = block.shape[1]
         cur = block[8 : 8 + rows]
@@ -99,16 +124,27 @@
         (m3r, m3i),
     )
     result = []
-    for wave in range(3):
+    for wave in range(2 if only_third else 0, 3):
         spread, strength = DIFFRACT[wave], COUPLE[wave]
         mr, mi = mixing[wave]
         result.append(moving[2 * wave] - spread * laplace[2 * wave + 1] - strength * mi)
         result.append(moving[2 * wave + 1] + spread * laplace[2 * wave] + strength * mr)
-    return current, result
+    return current[4:] if only_third else current, result
 
 
 def kernel(
     devices,
+    w1_hbm,
+    w2_hbm,
+    mis_hbm,
+    plate_hbm,
+    low_hbm,
+    high_hbm,
+    rgain_hbm,
+    cgain_hbm,
+    third_ref,
+    far_ref,
+    back_ref,
     w1_ref,
     w2_ref,
     mis_ref,
@@ -117,15 +153,6 @@
     high_ref,
     rgain_ref,
     cgain_ref,
-    lhigh_hbm,
-    llow_hbm,
-    thigh_hbm,
-    tlow_hbm,
-    shigh_hbm,
-    slow_hbm,
-    third_ref,
-    far_ref,
-    back_ref,
     lhigh,
     llow,
     thigh,
@@ -142,7 +169,7 @@
     g_in,
     h_out,
     h_in,
-    table_sem,
+    input_sem,
     edge_send,
     edge_recv,
     g_send,
@@ -163,20 +190,22 @@
     def place(index):
         return (index - devices // 2 + classes // 2) % classes
 
-    tables = [
-        pltpu.make_async_copy(src, dst, table_sem.at[i])
+    inputs = [
+        pltpu.make_async_copy(src, dst, input_sem.at[i])
         for i, (src, dst) in enumerate(
             (
-                (lhigh_hbm, lhigh),
-                (llow_hbm, llow),
-                (shigh_hbm, shigh),
-                (slow_hbm, slow),
-                (thigh_hbm, thigh),
-                (tlow_hbm, tlow),
+                (w1_hbm, w1_ref),
+                (w2_hbm, w2_ref),
+                (mis_hbm, mis_ref),
+                (plate_hbm, plate_ref),
+                (low_hbm, low_ref),
+                (high_hbm, high_ref),
+                (rgain_hbm, rgain_ref),
+                (cgain_hbm, cgain_ref),
             )
         )
     ]
-    for copy in tables:
+    for copy in inputs:
         copy.start()
 
     barrier = pltpu.get_barrier_semaphore()
@@ -186,6 +215,12 @@
         pl.semaphore_signal(
             barrier, inc=1, device_id={"gx": lax.rem(me + k, devices)}, device_id_type=MESH
         )
+
+    row_period = ZOOM * row_count
+    half = (far_rows // 2, row_count // 2)
+    wave_table(lhigh, llow, far_rows, row_count, half, row_period, (0, row_count))
+    for copy in inputs:
+        copy.wait()
 
     planes = [w1_ref[0], w1_ref[1], w2_ref[0], w2_ref[1], mis_ref[...]]
     own = PAD + HALO
@@ -225,6 +260,12 @@
     def _():
         edge_copy(1).start()
 
+    wave_table(
+        shigh, slow, far_columns, far_columns, (far_columns // 2,) * 2, far_columns,
+        (0, far_columns),
+    )
+    wave_table(thigh, tlow, row_count, far_rows, half[::-1], row_period, (row_count, 0))
+
     @pl.when(me > 0)
     def _():
         edge_copy(1).wait_recv()
@@ -268,7 +309,7 @@
     lowest = jnp.where(me == 0, HALO, 0)
     highest = jnp.where(me == devices - 1, HALO + width_here, wide)
 
-    def stage(source, position, finish):
+    def stage(source, position, finish, only_third=False):
         @pl.loop(0, tiles)
         def _(t):
             first = pl.multiple_of(t * TILE, 8)
@@ -278,11 +319,11 @@
             if position:
                 at = pl.ds(first, TILE)
                 turn = (turns[position - 1, 0, at, :], turns[position - 1, 1, at, :])
-            current, rate = rates(window, turn)
+            current, rate = rates(window, turn, only_third)
             row = first + lax.broadcasted_iota(jnp.int32, current[0].shape, 0)
             inside = (row >= lowest) & (row < highest)
-            for c in range(6):
-                finish(c, here, current[c], rate[c], inside)
+            for c, value, change in zip(range(6 - len(rate), 6), current, rate):
+                finish(c, here, value, change, inside)
 
     for substep in range(SUBSTEPS):
 
@@ -294,10 +335,10 @@
             fields[c, here, :] = jnp.where(inside, value, 0.0)
 
         stage(fields, substep, predict)
-        stage(trial, substep + 1, correct)
+        stage(trial, substep + 1, correct, substep == SUBSTEPS - 1)
 
     step = 2.0 * math.pi / LEVELS
-    plate_rows, plate_columns = plate_ref.shape
+    plate_columns, plate_rows = plate_ref.shape
 
     def phases(shape, rows_first):
         sub = lax.broadcasted_iota(jnp.int32, shape, 0)
@@ -306,7 +347,7 @@
         for r in range(plate_rows):
             for c in range(plate_columns):
                 at = (sub == r) & (lane == c) if rows_first else (sub == c) & (lane == r)
-                level = jnp.where(at, plate_ref[r, c], level)
+                level = jnp.where(at, plate_ref[c, r], level)
         angle = step * level.astype(jnp.float32)
         return jnp.cos(angle), jnp.sin(angle)
 
@@ -334,19 +375,6 @@
             axis=0,
         )
     )
-    tables[0].wait()
-    tables[1].wait()
-    chunks = max(1, far_rows // 128)
-    chunk = far_rows // chunks
-    per = chunk // block
-    for n in range(chunks):
-        at = slice(n * chunk, (n + 1) * chunk)
-        g = dot3((lhigh[at, :], llow[at, :]), near, True)
-        for j in range(per):
-            rows = slice(j * block, (j + 1) * block)
-            g_out[n * per + j, :block, :] = g[rows, :width_here]
-            g_out[n * per + j, block:, :] = g[rows, width_here:]
-
     def g_copy(target, source):
         return pltpu.make_async_remote_copy(
             src_ref=g_out.at[target],
@@ -357,9 +385,24 @@
             device_id_type=MESH,
         )
 
-    @pl.loop(1, devices)
-    def _(k):
-        g_copy(lax.rem(me + k, devices), me).start()
+    per = max(1, devices // 4)
+    chunk = per * block
+    for n in range(devices // per):
+        group = lax.rem(me // per + devices // per // 2 + n, devices // per)
+        at = pl.ds(pl.multiple_of(group * chunk, chunk), chunk)
+        g = dot3((lhigh[at, :], llow[at, :]), near, True)
+        for j in range(per):
+            rows = slice(j * block, (j + 1) * block)
+            target = group * per + j
+            g_out[target, :block, :] = g[rows, :width_here]
+            g_out[target, block:, :] = g[rows, width_here:]
+
+        for j in range(per):
+            target = group * per + j
+
+            @pl.when(target != me)
+            def _():
+                g_copy(target, me).start()
 
     g_in[me] = g_out[me]
     third_ref[0] = tr.T
@@ -375,8 +418,6 @@
     spot_low, spot_high, row_gain = pick(low_ref), pick(high_ref), pick(rgain_ref)
     gain = row_gain * cgain_ref[...]
 
-    tables[2].wait()
-    tables[3].wait()
 
     @pl.loop(1, devices)
     def _(k):
@@ -425,8 +466,6 @@
     h_in[me] = h_out[place(me)]
     down = phases((max(8, plate_rows), width_here), True)
     cosine, sine = (spread(v, plate_rows) for v in down)
-    tables[4].wait()
-    tables[5].wait()
 
     @pl.loop(1, devices)
     def _(k):
@@ -469,32 +508,10 @@
     block = far_rows // devices
     classes = far_columns // width_here
 
-    def angle_table(first, second, period):
-        turns = np.mod(first[:, None] * second[None, :], period)
-        angle = 2.0 * np.pi / period * turns
-        return np.cos(angle), np.sin(angle)
-
-    row_table = np.concatenate(
-        angle_table(
-            np.arange(far_rows) - far_rows // 2,
-            np.arange(row_count) - row_count // 2,
-            ZOOM * row_count,
-        ),
-        axis=1,
-    )
-    around = np.arange(far_columns) - far_columns // 2
-    column_table = np.concatenate(angle_table(around, around, far_columns), axis=1)
-    tables = (
-        *split_host(row_table),
-        *split_host(row_table.T),
-        *split_host(column_table),
-    )
-    tables = [jnp.asarray(t) for t in tables]
     wide = width_here + 2 * HALO
     vmem = pl.BlockSpec(memory_space=pltpu.VMEM)
-    smem = pl.BlockSpec(memory_space=pltpu.SMEM)
-    anywhere = pl.BlockSpec(memory_space=pl.ANY)
-    f32 = jnp.float32
+    hbm = pl.BlockSpec(memory_space=pltpu.HBM)
+    f32, bf16 = jnp.float32, jnp.bfloat16
     dma = pltpu.SemaphoreType.DMA
 
     def body(*refs):
@@ -507,10 +524,23 @@
             jax.ShapeDtypeStruct((2, block, far_columns), f32),
             jax.ShapeDtypeStruct((2, row_count, width_here), f32),
         ),
-        in_specs=[vmem] * 3 + [smem] + [vmem] * 4 + [anywhere] * 6,
+        in_specs=[hbm] * 8,
         out_specs=(vmem,) * 3,
         scratch_shapes=[
-            *[pltpu.VMEM(t.shape, t.dtype) for t in tables],
+            pltpu.VMEM((2, row_count, width_here), f32),
+            pltpu.VMEM((2, row_count, width_here), f32),
+            pltpu.VMEM((row_count, width_here), f32),
+            pltpu.SMEM(plate.shape[::-1], jnp.int32),
+            pltpu.VMEM((1, far_rows), jnp.int32),
+            pltpu.VMEM((1, far_rows), jnp.int32),
+            pltpu.VMEM((1, far_rows), f32),
+            pltpu.VMEM((1, far_columns), f32),
+            pltpu.VMEM((far_rows, 2 * row_count), bf16),
+            pltpu.VMEM((far_rows, 2 * row_count), bf16),
+            pltpu.VMEM((2 * row_count, far_rows), bf16),
+            pltpu.VMEM((2 * row_count, far_rows), bf16),
+            pltpu.VMEM((far_columns, 2 * far_columns), bf16),
+            pltpu.VMEM((far_columns, 2 * far_columns), bf16),
             pltpu.VMEM((6, wide + 2 * PAD, row_count), f32),
             pltpu.VMEM((6, wide + 2 * PAD, row_count), f32),
             pltpu.VMEM((SUBSTEPS, 2, wide, row_count), f32),
@@ -521,7 +551,7 @@
             pltpu.VMEM((devices, 2 * block, width_here), f32),
             pltpu.VMEM((classes, 2 * block, width_here), f32),
             pltpu.VMEM((devices, 2 * block, width_here), f32),
-            dma((6,)),
+            dma((8,)),
             dma((2,)),
             dma((2,)),
             dma((devices,)),
@@ -530,18 +560,17 @@
             dma((devices,)),
         ],
         compiler_params=pltpu.CompilerParams(
-            collective_id=0, has_side_effects=True, vmem_limit_bytes=48 * 1024 * 1024
+            collective_id=0, has_side_effects=True, vmem_limit_bytes=67043328
         ),
     )(
         wave_one,
         wave_two,
         mismatch,
-        plate,
+        plate.T,
         spot_low[None],
         spot_high[None],
         row_gain[None],
         column_gain[None],
-        *tables,
     )
 
 

time: 60.1 us -> 49.6 us (0.83)
  local copies, waits for them, and re-layouts: 12.9 us -> 3.09 us
    unnamed x32 -> x7, local copies, waits for them, and re-layouts: 12.9 us -> 3.09 us
where the time goes in v1:
time: 49.6 us; the launch traced here: 49.1 us
  Pallas kernels  45.4 us (92%)
  local copies, waits for them, and re-layouts  3.09 us (6%)
  between operations  0.66 us (1%)
    pallas_call x1, Pallas kernels, local(): pl.pallas_call(body, out_shape=(jax.ShapeDtypeStruct((2, row_count, width...  45.4 us
    unnamed x7, local copies, waits for them, and re-layouts  3.09 us

profile of v1, /device:TPU:13, one launch (start us, length us, event | category | flops | bytes accessed | tf_op | source)
XLA Modules:
  0.0 49.1 jit_solution(1232282350735521255)
XLA Ops:
  0.6 45.4 %shard_map.103 = (f32[2,256,128]{2,1,0:T(8,128)}, f32[2,32,512]{2,1,0:T(8,128)}, f32[2,256,128]{2,1,0:T(8,128)}) custom-call(f32[2,256,128]{2,1,0:T(8,128)} %refs_0_.1, f32[2,256,128]{2,1,0:T(8,128)} %refs_1_.1, f32[256,128]{1,0:T(8,128)} %refs_2_.1, s32[4,8]{1,0:T(4,128)} %bitcast.5, s32[1,512]{1,0:T(1,128)} %bitcast.6, s32[1,512]{1,0:T(1,128)} %bitcast.7, ...), custom_call_target="tpu_custom_call" | custom-call | tf_op jit(solution)/shard_map/pallas_call | solution.py:520
  46.0 0.0 copy-start.1
  46.0 0.0 copy-start
  46.1 1.7 %copy.14 = f32[2,256,128]{2,1,0:T(8,128)} copy(f32[2,256,128]{2,1,0:T(8,128)} %get-tuple-element.6) | data formatting | bytes 524288
  47.8 0.0 copy-done.1
  47.8 0.7 %copy.15 = f32[2,32,512]{2,1,0:T(8,128)} copy(f32[2,32,512]{2,1,0:T(8,128)S(1)} %copy-done.1) | data formatting | bytes 262144
  48.4 0.0 copy-done
  48.4 0.7 %copy.16 = f32[2,256,128]{2,1,0:T(8,128)} copy(f32[2,256,128]{2,1,0:T(8,128)S(1)} %copy-done) | data formatting | bytes 524288
Async XLA Ops:
  46.0 1.7 %copy-start.1 = (f32[2,32,512]{2,1,0:T(8,128)S(1)}, f32[2,32,512]{2,1,0:T(8,128)}, u32[]{:S(2)}) copy-start(f32[2,32,512]{2,1,0:T(8,128)} %get-tuple-element.7) | copy-start | bytes 393220
  46.0 2.4 %copy-start = (f32[2,256,128]{2,1,0:T(8,128)S(1)}, f32[2,256,128]{2,1,0:T(8,128)}, u32[]{:S(2)}) copy-start(f32[2,256,128]{2,1,0:T(8,128)} %get-tuple-element.8) | copy-start | bytes 786436

commit v2 on v1

--- a/solution.py
+++ b/solution.py
@@ -185,7 +185,8 @@
     classes = far_columns // width_here
     scale = FAR_SCALE / math.sqrt(row_count * width_here * devices)
     wide = width_here + 2 * HALO
-    tiles = wide // TILE
+    half_width = width_here // 2
+    half_rows = half_width + 2 * HALO
 
     def place(index):
         return (index - devices // 2 + classes // 2) % classes
@@ -217,28 +218,34 @@
         )
 
     row_period = ZOOM * row_count
-    half = (far_rows // 2, row_count // 2)
-    wave_table(lhigh, llow, far_rows, row_count, half, row_period, (0, row_count))
+    middle = (far_rows // 2, row_count // 2)
+    wave_table(lhigh, llow, far_rows, row_count, middle, row_period, (0, row_count))
     for copy in inputs:
         copy.wait()
 
     planes = [w1_ref[0], w1_ref[1], w2_ref[0], w2_ref[1], mis_ref[...]]
     own = PAD + HALO
+    kept = half_width + HALO
     for plane, value in enumerate(planes):
         turned = value.T
         edge_out[0, plane * HALO : (plane + 1) * HALO, :] = turned[:HALO]
         edge_out[1, plane * HALO : (plane + 1) * HALO, :] = turned[width_here - HALO :]
         if plane < 4:
-            fields[plane, own : own + width_here, :] = turned
+            fields[0, plane, own : own + kept, :] = turned[:kept]
+            fields[1, plane, PAD : PAD + kept, :] = turned[width_here - kept :]
         else:
             mis_wide[HALO : HALO + width_here, :] = turned
-    for plane in (4, 5):
-        fields[plane] = jnp.zeros(fields.shape[1:], jnp.float32)
     edge = jnp.zeros((PAD, row_count), jnp.float32)
     for plane in range(6):
-        for start in (0, PAD + wide):
-            fields[plane, start : start + PAD, :] = edge
+        for start in (0, PAD + half_rows):
             trial[plane, start : start + PAD, :] = edge
+            for h in range(2):
+                fields[h, plane, start : start + PAD, :] = edge
+    for h in range(2):
+        for plane in (4, 5):
+            fields[h, plane, PAD : PAD + half_rows, :] = jnp.zeros(
+                (half_rows, row_count), jnp.float32
+            )
 
     pl.semaphore_wait(barrier, devices - 1)
 
@@ -264,78 +271,79 @@
         shigh, slow, far_columns, far_columns, (far_columns // 2,) * 2, far_columns,
         (0, far_columns),
     )
-    wave_table(thigh, tlow, row_count, far_rows, half[::-1], row_period, (row_count, 0))
-
-    @pl.when(me > 0)
-    def _():
-        edge_copy(1).wait_recv()
-
-    @pl.when(me == 0)
-    def _():
-        edge_in[0] = jnp.zeros(edge_in.shape[1:], jnp.float32)
-
-    @pl.when(me < devices - 1)
-    def _():
-        edge_copy(0).wait_recv()
-
-    @pl.when(me == devices - 1)
-    def _():
-        edge_in[1] = jnp.zeros(edge_in.shape[1:], jnp.float32)
-
-    for side, start in ((0, 0), (1, HALO + width_here)):
+    wave_table(thigh, tlow, row_count, far_rows, middle[::-1], row_period, (row_count, 0))
+
+    def take_edge(side):
+        there = me > 0 if side == 0 else me < devices - 1
+
+        @pl.when(there)
+        def _():
+            edge_copy(1 - side).wait_recv()
+
+        @pl.when(jnp.logical_not(there))
+        def _():
+            edge_in[side] = jnp.zeros(edge_in.shape[1:], jnp.float32)
+
+        start = 0 if side == 0 else HALO + width_here
+        at = PAD + start - side * half_width
         for plane in range(5):
             value = edge_in[side, plane * HALO : (plane + 1) * HALO, :]
             if plane < 4:
-                fields[plane, PAD + start : PAD + start + HALO, :] = value
+                fields[side, plane, at : at + HALO, :] = value
             else:
                 mis_wide[start : start + HALO, :] = value
 
-    @pl.loop(0, tiles)
-    def _(t):
-        here = pl.ds(pl.multiple_of(t * TILE, TILE), TILE)
-        sine, cosine = sine_cosine(mis_wide[here, :])
-        c2 = cosine * cosine - sine * sine
-        s2 = 2.0 * sine * cosine
-        powers = (
-            (cosine, sine),
-            (c2, s2),
-            (c2 * cosine - s2 * sine, s2 * cosine + c2 * sine),
-            (c2 * c2 - s2 * s2, 2.0 * s2 * c2),
-        )
-        for z, (c, s) in enumerate(powers):
-            turns[z, 0, here, :] = c
-            turns[z, 1, here, :] = s
+        start = side * half_rows
+        count = half_rows if side == 0 else wide - half_rows
+
+        @pl.loop(start // TILE, (start + count) // TILE)
+        def _(t):
+            here = pl.ds(pl.multiple_of(t * TILE, TILE), TILE)
+            sine, cosine = sine_cosine(mis_wide[here, :])
+            c2 = cosine * cosine - sine * sine
+            s2 = 2.0 * sine * cosine
+            powers = (
+                (cosine, sine),
+                (c2, s2),
+                (c2 * cosine - s2 * sine, s2 * cosine + c2 * sine),
+                (c2 * c2 - s2 * s2, 2.0 * s2 * c2),
+            )
+            for z, (c, s) in enumerate(powers):
+                turns[z, 0, here, :] = c
+                turns[z, 1, here, :] = s
 
     lowest = jnp.where(me == 0, HALO, 0)
     highest = jnp.where(me == devices - 1, HALO + width_here, wide)
 
-    def stage(source, position, finish, only_third=False):
-        @pl.loop(0, tiles)
+    def stage(source, shift, position, finish, only_third=False):
+        @pl.loop(0, half_rows // TILE)
         def _(t):
             first = pl.multiple_of(t * TILE, 8)
             here = pl.ds(pl.multiple_of(first + PAD, 8), TILE)
             window = [source[c, pl.ds(first, TILE + 16), :] for c in range(6)]
             turn = None
             if position:
-                at = pl.ds(first, TILE)
+                at = pl.ds(pl.multiple_of(first + shift, 8), TILE)
                 turn = (turns[position - 1, 0, at, :], turns[position - 1, 1, at, :])
             current, rate = rates(window, turn, only_third)
-            row = first + lax.broadcasted_iota(jnp.int32, current[0].shape, 0)
+            row = first + shift + lax.broadcasted_iota(jnp.int32, current[0].shape, 0)
             inside = (row >= lowest) & (row < highest)
             for c, value, change in zip(range(6 - len(rate), 6), current, rate):
                 finish(c, here, value, change, inside)
 
-    for substep in range(SUBSTEPS):
-
-        def predict(c, here, current, rate, inside):
-            trial[c, here, :] = jnp.where(inside, current + rate, 0.0)
-
-        def correct(c, here, current, rate, inside):
-            value = 0.5 * (fields[c, here, :] + (current + rate))
-            fields[c, here, :] = jnp.where(inside, value, 0.0)
-
-        stage(fields, substep, predict)
-        stage(trial, substep + 1, correct, substep == SUBSTEPS - 1)
+    def crystal(h):
+        for substep in range(SUBSTEPS):
+
+            def predict(c, here, current, rate, inside):
+                trial[c, here, :] = jnp.where(inside, current + rate, 0.0)
+
+            def correct(c, here, current, rate, inside):
+                value = 0.5 * (fields[h, c, here, :] + (current + rate))
+                fields[h, c, here, :] = jnp.where(inside, value, 0.0)
+
+            shift = h * half_width
+            stage(fields.at[h], shift, substep, predict)
+            stage(trial, shift, substep + 1, correct, substep == SUBSTEPS - 1)
 
     step = 2.0 * math.pi / LEVELS
     plate_columns, plate_rows = plate_ref.shape
@@ -362,51 +370,54 @@
 
     across = phases((max(8, plate_columns), row_count), False)
     cosine, sine = (spread(v, plate_columns) for v in across)
-    tr = fields[4, own : own + width_here, :]
-    ti = fields[5, own : own + width_here, :]
-    nr = tr * cosine - ti * sine
-    ni = tr * sine + ti * cosine
-    near = split(
-        jnp.concatenate(
-            [
-                jnp.concatenate([nr, ni], axis=1),
-                jnp.concatenate([ni, -nr], axis=1),
-            ],
-            axis=0,
-        )
-    )
-    def g_copy(target, source):
+    def g_copy(h, target, source):
         return pltpu.make_async_remote_copy(
-            src_ref=g_out.at[target],
-            dst_ref=g_in.at[source],
-            send_sem=g_send.at[target],
-            recv_sem=g_recv.at[source],
+            src_ref=g_out.at[h, target],
+            dst_ref=g_in.at[h, source],
+            send_sem=g_send.at[h, target],
+            recv_sem=g_recv.at[h, source],
             device_id={"gx": target},
             device_id_type=MESH,
         )
 
     per = max(1, devices // 4)
     chunk = per * block
-    for n in range(devices // per):
-        group = lax.rem(me // per + devices // per // 2 + n, devices // per)
-        at = pl.ds(pl.multiple_of(group * chunk, chunk), chunk)
-        g = dot3((lhigh[at, :], llow[at, :]), near, True)
-        for j in range(per):
-            rows = slice(j * block, (j + 1) * block)
-            target = group * per + j
-            g_out[target, :block, :] = g[rows, :width_here]
-            g_out[target, block:, :] = g[rows, width_here:]
-
-        for j in range(per):
-            target = group * per + j
-
-            @pl.when(target != me)
-            def _():
-                g_copy(target, me).start()
-
-    g_in[me] = g_out[me]
-    third_ref[0] = tr.T
-    third_ref[1] = ti.T
+    for h in range(2):
+        take_edge(h)
+        crystal(h)
+        tr = fields[h, 4, own : own + half_width, :]
+        ti = fields[h, 5, own : own + half_width, :]
+        turn = [v[h * half_width : (h + 1) * half_width] for v in (cosine, sine)]
+        nr = tr * turn[0] - ti * turn[1]
+        ni = tr * turn[1] + ti * turn[0]
+        near = split(
+            jnp.concatenate(
+                [
+                    jnp.concatenate([nr, ni], axis=1),
+                    jnp.concatenate([ni, -nr], axis=1),
+                ],
+                axis=0,
+            )
+        )
+        for n in range(devices // per):
+            group = lax.rem(me // per + devices // per // 2 + n, devices // per)
+            at = pl.ds(pl.multiple_of(group * chunk, chunk), chunk)
+            g = dot3((lhigh[at, :], llow[at, :]), near, True)
+            for j in range(per):
+                g_out[h, group * per + j] = g[j * block : (j + 1) * block]
+
+            for j in range(per):
+                target = group * per + j
+
+                @pl.when(target != me)
+                def _():
+                    g_copy(h, target, me).start()
+
+        g_in[h, me] = g_out[h, me]
+
+    for part in range(2):
+        ends = [fields[h, 4 + part, own : own + half_width, :] for h in range(2)]
+        third_ref[part] = jnp.concatenate(ends, axis=0).T
 
     lane = lax.broadcasted_iota(jnp.int32, (block, far_rows), 1)
     row = me * block + lax.broadcasted_iota(jnp.int32, (block, far_rows), 0)
@@ -422,16 +433,22 @@
     @pl.loop(1, devices)
     def _(k):
         source = lax.rem(me + k, devices)
-        g_copy(source, source).wait_recv()
-
-    folded = []
+        g_copy(0, source, source).wait_recv()
+        g_copy(1, source, source).wait_recv()
+
+    real, imaginary = [], []
     for position in range(classes):
-        total = None
-        for source in range(devices):
-            if place(source) == position:
-                total = g_in[source] if total is None else total + g_in[source]
-        folded.append(total)
-    spectrum = dot3(split(jnp.concatenate(folded, axis=1)), (shigh[...], slow[...]))
+        for h in range(2):
+            total = None
+            for source in range(devices):
+                if place(source) == position:
+                    total = g_in[h, source] if total is None else total + g_in[h, source]
+            real.append(total[:, :half_width])
+            imaginary.append(total[:, half_width:])
+    folded = jnp.concatenate(
+        [jnp.concatenate(real, axis=1), jnp.concatenate(imaginary, axis=1)], axis=0
+    )
+    spectrum = dot3(split(folded), (shigh[...], slow[...]))
     far_r = scale * (spectrum[:block, :far_columns] + spectrum[block:, far_columns:])
     far_i = scale * (spectrum[block:, :far_columns] - spectrum[:block, far_columns:])
     far_ref[0] = far_r
@@ -467,19 +484,28 @@
     down = phases((max(8, plate_rows), width_here), True)
     cosine, sine = (spread(v, plate_rows) for v in down)
 
-    @pl.loop(1, devices)
-    def _(k):
-        source = lax.rem(me + k, devices)
-        h_copy(source, source).wait_recv()
-
-    gathered = jnp.concatenate(
-        [
-            jnp.concatenate([h_in[s, :block, :], h_in[s, block:, :]], axis=1)
-            for s in range(devices)
-        ],
-        axis=0,
-    )
-    summed = dot3((thigh[...], tlow[...]), split(gathered))
+    count = devices // 2
+    summed = None
+    for n in range(2):
+        group = lax.rem(me // count + n, 2)
+
+        @pl.loop(0, count)
+        def _(k):
+            source = group * count + k
+
+            @pl.when(source != me)
+            def _():
+                h_copy(source, source).wait_recv()
+
+        gathered = []
+        for k in range(count):
+            value = h_in[group * count + k]
+            gathered.append(jnp.concatenate([value[:block], value[block:]], axis=1))
+        at = pl.ds(pl.multiple_of(group * count * block, count * block), count * block)
+        part = dot3(
+            (thigh[:, at], tlow[:, at]), split(jnp.concatenate(gathered, axis=0))
+        )
+        summed = part if summed is None else summed + part
     br = scale * (summed[:row_count, :width_here] - summed[row_count:, width_here:])
     bi = scale * (summed[:row_count, width_here:] + summed[row_count:, :width_here])
     back_ref[0] = br * cosine + bi * sine
@@ -496,7 +522,8 @@
     @pl.loop(1, devices)
     def _(k):
         target = lax.rem(me + k, devices)
-        g_copy(target, me).wait_send()
+        g_copy(0, target, me).wait_send()
+        g_copy(1, target, me).wait_send()
         h_copy(target, me).wait_send()
 
 
@@ -509,6 +536,7 @@
     classes = far_columns // width_here
 
     wide = width_here + 2 * HALO
+    half_rows = width_here // 2 + 2 * HALO
     vmem = pl.BlockSpec(memory_space=pltpu.VMEM)
     hbm = pl.BlockSpec(memory_space=pltpu.HBM)
     f32, bf16 = jnp.float32, jnp.bfloat16
@@ -541,21 +569,21 @@
             pltpu.VMEM((2 * row_count, far_rows), bf16),
             pltpu.VMEM((far_columns, 2 * far_columns), bf16),
             pltpu.VMEM((far_columns, 2 * far_columns), bf16),
-            pltpu.VMEM((6, wide + 2 * PAD, row_count), f32),
-            pltpu.VMEM((6, wide + 2 * PAD, row_count), f32),
+            pltpu.VMEM((2, 6, half_rows + 2 * PAD, row_count), f32),
+            pltpu.VMEM((6, half_rows + 2 * PAD, row_count), f32),
             pltpu.VMEM((SUBSTEPS, 2, wide, row_count), f32),
             pltpu.VMEM((2, 5 * HALO, row_count), f32),
             pltpu.VMEM((2, 5 * HALO, row_count), f32),
             pltpu.VMEM((wide, row_count), f32),
-            pltpu.VMEM((devices, 2 * block, width_here), f32),
-            pltpu.VMEM((devices, 2 * block, width_here), f32),
+            pltpu.VMEM((2, devices, block, width_here), f32),
+            pltpu.VMEM((2, devices, block, width_here), f32),
             pltpu.VMEM((classes, 2 * block, width_here), f32),
             pltpu.VMEM((devices, 2 * block, width_here), f32),
             dma((8,)),
             dma((2,)),
             dma((2,)),
-            dma((devices,)),
-            dma((devices,)),
+            dma((2, devices)),
+            dma((2, devices)),
             dma((devices,)),
             dma((devices,)),
         ],

time: 49.6 us -> 46.2 us (0.931)
  Pallas kernels: 45.4 us -> 42.3 us
    pallas_call x1, Pallas kernels: 45.4 us -> 42.3 us  [local(): pl.pallas_call(body, out_shape=(jax.ShapeDtypeStruct((2, row_count, width...]
where the time goes in v2:
time: 46.2 us; the launch traced here: 46 us
  Pallas kernels  42.3 us (92%)
  local copies, waits for them, and re-layouts  3.09 us (7%)
  between operations  0.66 us (1%)
    pallas_call x1, Pallas kernels, local(): pl.pallas_call(body, out_shape=(jax.ShapeDtypeStruct((2, row_count, width...  42.3 us
    unnamed x7, local copies, waits for them, and re-layouts  3.09 us

profile of v2, /device:TPU:13, one launch (start us, length us, event | category | flops | bytes accessed | tf_op | source)
XLA Modules:
  0.0 46.0 jit_solution(6638719113621544179)
XLA Ops:
  0.6 42.3 %shard_map.103 = (f32[2,256,128]{2,1,0:T(8,128)}, f32[2,32,512]{2,1,0:T(8,128)}, f32[2,256,128]{2,1,0:T(8,128)}) custom-call(f32[2,256,128]{2,1,0:T(8,128)} %refs_0_.1, f32[2,256,128]{2,1,0:T(8,128)} %refs_1_.1, f32[256,128]{1,0:T(8,128)} %refs_2_.1, s32[4,8]{1,0:T(4,128)} %bitcast.5, s32[1,512]{1,0:T(1,128)} %bitcast.6, s32[1,512]{1,0:T(1,128)} %bitcast.7, ...), custom_call_target="tpu_custom_call" | custom-call | tf_op jit(solution)/shard_map/pallas_call | solution.py:548
  42.9 0.0 copy-start.1
  43.0 0.0 copy-start
  43.0 1.7 %copy.14 = f32[2,256,128]{2,1,0:T(8,128)} copy(f32[2,256,128]{2,1,0:T(8,128)} %get-tuple-element.6) | data formatting | bytes 524288
  44.7 0.0 copy-done.1
  44.7 0.7 %copy.15 = f32[2,32,512]{2,1,0:T(8,128)} copy(f32[2,32,512]{2,1,0:T(8,128)S(1)} %copy-done.1) | data formatting | bytes 262144
  45.3 0.0 copy-done
  45.3 0.7 %copy.16 = f32[2,256,128]{2,1,0:T(8,128)} copy(f32[2,256,128]{2,1,0:T(8,128)S(1)} %copy-done) | data formatting | bytes 524288
Async XLA Ops:
  42.9 1.7 %copy-start.1 = (f32[2,32,512]{2,1,0:T(8,128)S(1)}, f32[2,32,512]{2,1,0:T(8,128)}, u32[]{:S(2)}) copy-start(f32[2,32,512]{2,1,0:T(8,128)} %get-tuple-element.7) | copy-start | bytes 393220
  43.0 2.4 %copy-start = (f32[2,256,128]{2,1,0:T(8,128)S(1)}, f32[2,256,128]{2,1,0:T(8,128)}, u32[]{:S(2)}) copy-start(f32[2,256,128]{2,1,0:T(8,128)} %get-tuple-element.8) | copy-start | bytes 786436
